TPU v7x, 256 devices: a whole 4x4x8 slice. The times are simulated.
256 devices in a mesh: dp: 16 (over y, x), expert: 16 (over z, core).
Axes of the slice: x: 4, y: 4, z: 8, core: 2. Of those that a mesh axis runs over, the one named last changes fastest.
Arguments:
- tokens: bfloat16 [32768, 1024], P(('dp', 'expert')), may hold values from -6 to 6
- cotangent: bfloat16 [32768, 1024], P(('dp', 'expert')), may hold values from -6 to 6
- expert_ids: int32 [32768, 8], P(('dp', 'expert')), may hold values from 0 to 31, all different within a row; in each aligned block of 128 rows (0 to 127, 128 to 255, ...) at most 40 rows name the same one
- gate_probs: bfloat16 [32768, 8], P(('dp', 'expert')), may hold values from 0.049804688 to 0.5
- gate_up: bfloat16 [32, 1024, 1024], P('expert', 'dp'), may hold values from -0.1875 to 0.1875
- down_proj: bfloat16 [32, 512, 1024], P('expert', 'dp'), may hold values from -0.25 to 0.25
Outputs:
- grad_tokens: bfloat16 [32768, 1024], P(('dp', 'expert'))
- grad_gates: bfloat16 [32768, 8], P(('dp', 'expert'))
- grad_gate_up: float32 [32, 1024, 1024], P('expert', 'dp')
- grad_down: float32 [32, 512, 1024], P('expert', 'dp')
Inputs may be any that keep to these rules, and one draw needn't show every extreme that they name: `expert_ids`: each token names 8 different experts. Among the 128 tokens of one device (aligned blocks of rows) no expert is named more than 40 times, and in every draw some expert is named exactly 40 times by the tokens of some device.
All inputs are finite; a program needn't handle non-finite values.
Results may differ from a plain program's by a relative error of at most 0.0058.
Values may be sent and summed in bfloat16 or wider, within the bound.
No kernel may reach another device: no remote copies, remote signals or barrier semaphores. Data moves between devices by JAX's collectives and lax.ppermute only.
A program may use at most 128 MiB of HBM per device.

v0:
```python
import jax
import jax.numpy as jnp
from jax import lax
from jax.sharding import PartitionSpec as P

TOP = 8
EXP_DEV = 2


def slot_index(expert_ids, experts_all, capacity):
    flat_ids = expert_ids.reshape(-1)
    onehot = (flat_ids[:, None] == jnp.arange(experts_all, dtype=jnp.int32)[None, :]).astype(
        jnp.int32
    )
    before = jnp.cumsum(onehot, axis=0) - onehot
    slot_rank = jnp.sum(before * onehot, axis=1)
    return flat_ids * capacity + slot_rank


def expert_grads(routed_x, routed_dy, routed_gate, w_in, w_out):
    pre_act = jnp.einsum("jrd,jdf->jrf", routed_x, w_in, preferred_element_type=jnp.float32)
    hidden = w_out.shape[1]
    gate_pre = pre_act[..., :hidden]
    up_pre = pre_act[..., hidden:]
    sigmoid_h = jax.nn.sigmoid(gate_pre)
    silu_h = gate_pre * sigmoid_h
    activation = silu_h * up_pre
    raw_grad = jnp.einsum("jrd,jfd->jrf", routed_dy, w_out, preferred_element_type=jnp.float32)
    gate_col = routed_gate.astype(jnp.float32)[..., None]
    act_grad = gate_col * raw_grad
    grad_gate = act_grad * up_pre * sigmoid_h * (1.0 + gate_pre * (1.0 - sigmoid_h))
    grad_up = act_grad * silu_h
    pre_grad = jnp.concatenate([grad_gate, grad_up], axis=-1).astype(jnp.bfloat16)
    scaled_act = (gate_col * activation).astype(jnp.bfloat16)
    slot_dx = jnp.einsum("jrf,jdf->jrd", pre_grad, w_in, preferred_element_type=jnp.float32).astype(
        jnp.bfloat16
    )
    slot_gate = jnp.sum(activation * raw_grad, axis=-1).astype(jnp.bfloat16)
    return (pre_grad, scaled_act, slot_dx, slot_gate)


def row_terms(left_side, right_side, row_count):
    summed = jnp.einsum("jrc,jrf->cjf", left_side, right_side, preferred_element_type=jnp.float32)
    return summed.reshape(row_count, -1)


def body(tokens, cotangent, expert_ids, gate_probs, gate_up, down_proj):
    tok_count, width = tokens.shape
    owners = lax.axis_size("expert")
    experts_all = EXP_DEV * owners
    capacity = 5 * tok_count * TOP // (4 * experts_all)
    slot_dest = slot_index(expert_ids, experts_all, capacity)
    buffer_rows = experts_all * capacity
    send_x = (
        jnp.zeros((buffer_rows, width), jnp.bfloat16)
        .at[slot_dest]
        .set(jnp.repeat(tokens, TOP, axis=0))
    )
    send_dy = (
        jnp.zeros((buffer_rows, width), jnp.bfloat16)
        .at[slot_dest]
        .set(jnp.repeat(cotangent, TOP, axis=0))
    )
    send_gate = jnp.zeros((buffer_rows,), jnp.bfloat16).at[slot_dest].set(gate_probs.reshape(-1))
    block_shape = (owners, EXP_DEV, capacity, width)
    recv_x, recv_dy, recv_gate = (
        lax.all_to_all(
            send_x.reshape(block_shape), "expert", split_axis=0, concat_axis=2, tiled=True
        ),
        lax.all_to_all(
            send_dy.reshape(block_shape), "expert", split_axis=0, concat_axis=2, tiled=True
        ),
        lax.all_to_all(
            send_gate.reshape(owners, EXP_DEV, capacity),
            "expert",
            split_axis=0,
            concat_axis=2,
            tiled=True,
        ),
    )
    routed_x = recv_x[0]
    routed_dy = recv_dy[0]
    routed_gate = recv_gate[0]
    rows_in = gate_up.shape[1]
    rows_out = down_proj.shape[1]
    w_in, w_out = (
        lax.all_gather(gate_up, "dp", axis=1, tiled=True),
        lax.all_gather(down_proj, "dp", axis=1, tiled=True),
    )
    pre_grad, scaled_act, slot_dx, slot_gate = expert_grads(
        routed_x, routed_dy, routed_gate, w_in, w_out
    )
    summed_in = lax.psum_scatter(
        row_terms(routed_x, pre_grad, rows_in * lax.axis_size("dp")),
        "dp",
        scatter_dimension=0,
        tiled=True,
    )
    summed_out = lax.psum_scatter(
        row_terms(scaled_act, routed_dy, rows_out * lax.axis_size("dp")),
        "dp",
        scatter_dimension=0,
        tiled=True,
    )
    grad_gate_up = summed_in.reshape(rows_in, EXP_DEV, -1).transpose(1, 0, 2)
    grad_down = summed_out.reshape(rows_out, EXP_DEV, -1).transpose(1, 0, 2)
    back_dx, back_gate = (
        lax.all_to_all(slot_dx[None], "expert", split_axis=2, concat_axis=0, tiled=True),
        lax.all_to_all(slot_gate[None], "expert", split_axis=2, concat_axis=0, tiled=True),
    )
    slot_rows = back_dx.reshape(buffer_rows, width)[slot_dest]
    grad_tokens = jnp.sum(
        slot_rows.reshape(tok_count, TOP, width).astype(jnp.float32), axis=1
    ).astype(jnp.bfloat16)
    grad_gates = back_gate.reshape(buffer_rows)[slot_dest].reshape(tok_count, TOP)
    return (grad_tokens, grad_gates, grad_gate_up, grad_down)


def solution(mesh):
    placed = (
        P(("dp", "expert"), None),
        P(("dp", "expert"), None),
        P(("dp", "expert"), None),
        P(("dp", "expert"), None),
        P("expert", "dp", None),
        P("expert", "dp", None),
    )
    return jax.shard_map(
        body,
        mesh=mesh,
        in_specs=placed,
        out_specs=(
            P(("dp", "expert"), None),
            P(("dp", "expert"), None),
            P("expert", "dp", None),
            P("expert", "dp", None),
        ),
        check_vma=False,
    )
```

profile of v0, /device:TPU:24, one launch (start us, length us, event | category | flops | bytes accessed | tf_op | source)
XLA Modules:
  0.0 380.2 jit_solution(4605365207191000770)
XLA Ops:
  7.2 0.0 copy-start
  7.2 0.0 all-gather.5.cloned.1.call-start
  7.2 0.7 all-gather.5.cloned.1.call-update
  7.9 0.7 broadcast_multiply_fusion
  8.6 0.8 copy.80
  9.4 0.1 eq.29
  9.5 0.1 eq.25
  9.6 0.8 copy.84
  10.4 0.1 reshape.155
  10.5 0.1 copy.79
  10.6 0.1 mul.59
  10.7 9.0 %reduce-window.6 = s32[32,8,128]{2,1,0:T(8,128)S(1)} reduce-window(s32[32,8,128]{2,1,0:T(8,128)S(1)} %fusion.15, s32[]{:T(128)} %constant.8.clone.1), window={size=1x1x128 pad=0_0x0_0x127_0}, to_apply=%region_0.0 | reduce-window | flops 4161536 | bytes 262148 | tf_op jit(solution)/shard_map/reduce-window
  19.7 0.1 slice.20
  19.8 0.1 copy.82
  20.0 0.1 copy.83
  20.1 0.1 broadcast_add_fusion
  20.2 7.6 %scatter_custom_fusion = bf16[1280]{0:T(1024)(128)(2,1)S(1)} fusion(s32[1024]{0:T(1024)S(1)} %bitcast.92, bf16[1024]{0:T(1024)(128)(2,1)S(1)} %reshape.155, bf16[]{:T(256)} %constant.6.clone.1), kind=kCustom, calls=%fused_computation.39 | custom fusion | bytes 2562 | tf_op jit(solution)/shard_map/scatter | solution.py:64
  27.8 0.7 reshape.120
  28.5 8.6 %all-to-all-start = ((bf16[16,2,40]{2,1,0:T(2,128)(2,1)}), bf16[16,2,40]{2,1,0:T(2,128)(2,1)S(1)}, u32[]{:S(2)}, u32[]{:S(2)}) async-start(bf16[16,2,40]{2,1,0:T(2,128)(2,1)} %reshape.120), calls=%async_computation | async-start | bytes 16384 | tf_op jit(solution)/shard_map/all_to_all | solution.py:73
  37.1 7.1 %scatter_custom_fusion.2 = bf16[1280,1024]{1,0:T(8,128)(2,1)} fusion(s32[1024]{0:T(1024)S(1)} %bitcast.93, bf16[]{:T(256)} %constant.6.clone.1, bf16[128,1024]{1,0:T(8,128)(2,1)S(1)} %copy-done), kind=kCustom, calls=%fused_computation.15 | custom fusion | bytes 2883586 | tf_op jit(solution)/shard_map/scatter | solution.py:57
  44.2 0.4 all-to-all-done
  44.6 7.0 %all-to-all-start.2 = ((bf16[16,2,40,1024]{3,2,1,0:T(8,128)(2,1)}), bf16[16,2,40,1024]{3,2,1,0:T(8,128)(2,1)S(1)}, u32[]{:S(2)}, u32[]{:S(2)}) async-start(bf16[16,2,40,1024]{3,2,1,0:T(8,128)(2,1)} %bitcast.79), calls=%async_computation.2 | async-start | bytes 5242880 | tf_op jit(solution)/shard_map/all_to_all | solution.py:67
  51.6 7.1 %scatter_custom_fusion.1 = bf16[1280,1024]{1,0:T(8,128)(2,1)} fusion(s32[1024]{0:T(1024)S(1)} %bitcast.94, bf16[]{:T(256)} %constant.6.clone.1, bf16[128,1024]{1,0:T(8,128)(2,1)S(1)} %copy-done.5), kind=kCustom, calls=%fused_computation.17 | custom fusion | bytes 2883586 | tf_op jit(solution)/shard_map/scatter | solution.py:62
  58.7 53.4 %all-to-all-done.2 = bf16[16,2,40,1024]{3,2,1,0:T(8,128)(2,1)S(1)} async-done(((bf16[16,2,40,1024]{3,2,1,0:T(8,128)(2,1)}), bf16[16,2,40,1024]{3,2,1,0:T(8,128)(2,1)S(1)}, u32[]{:S(2)}, u32[]{:S(2)}) %all-to-all-start.2) | async-done | bytes 2621472 | tf_op jit(solution)/shard_map/all_to_all | solution.py:67
  112.2 4.6 %all-to-all-start.1 = ((bf16[16,2,40,1024]{3,2,1,0:T(8,128)(2,1)}), bf16[16,2,40,1024]{3,2,1,0:T(8,128)(2,1)}, u32[]{:S(2)}, u32[]{:S(2)}) async-start(bf16[16,2,40,1024]{3,2,1,0:T(8,128)(2,1)} %bitcast.77), calls=%async_computation.1 | async-start | bytes 5242880 | tf_op jit(solution)/shard_map/all_to_all | solution.py:70
  116.8 0.0 all-gather.3.cloned.1.call-start
  116.9 0.7 all-gather.3.cloned.1.call-update
  117.6 0.0 reduce-scatter.5.cloned.1.call-start
  117.6 0.1 reshape.133
  117.7 1.8 copy.87
  119.5 57.9 %all-to-all-done.1 = bf16[16,2,40,1024]{3,2,1,0:T(8,128)(2,1)} async-done(((bf16[16,2,40,1024]{3,2,1,0:T(8,128)(2,1)}), bf16[16,2,40,1024]{3,2,1,0:T(8,128)(2,1)}, u32[]{:S(2)}, u32[]{:S(2)}) %all-to-all-start.1) | async-done | bytes 2621472 | tf_op jit(solution)/shard_map/all_to_all | solution.py:70
  177.4 3.7 copy.86
  181.1 5.6 %fusion.21 = f32[2,640,1024]{1,2,0:T(8,128)S(1)} fusion(bf16[2,640,1024]{2,1,0:T(8,128)(2,1)S(1)} %bitcast.82, bf16[2,1024,1024]{2,1,0:T(8,128)(2,1)} %all-gather.5.cloned.1.call-done), kind=kOutput, calls=%fused_computation.43 | convolution fusion | flops 2684354560 | bytes 12058624 | tf_op jit(solution)/shard_map/jrd,jdf->jrf/dot_general | solution.py:21
  186.7 4.5 %fusion.6 = f32[2,1024,512]{2,1,0:T(8,128)} fusion(bf16[2,640,1024]{2,1,0:T(8,128)(2,1)S(1)} %bitcast.85, f32[2,640]{1,0:T(2,128)S(1)} %reshape.133, f32[2,640,1024]{1,2,0:T(8,128)S(1)} %fusion.21), kind=kOutput, calls=%fused_computation.20 | convolution fusion | flops 1346764800 | bytes 12063744 | tf_op jit(solution)/shard_map/jrc,jrf->cjf/dot_general | solution.py:43
  191.2 5.4 %copy.99 = f32[512,2048]{1,0:T(8,128)} copy(f32[512,2048]{0,1:T(8,128)} %bitcast.81) | data formatting | bytes 8388608 | tf_op jit(solution)/shard_map/reshape | solution.py:44
  196.6 0.0 reduce-scatter.5.cloned.1.call-update
  196.6 0.0 reduce-scatter.3.cloned.1.call-start
  196.6 0.0 all-gather.3.cloned.1.call-done
  196.7 6.7 %multiply_convert_fusion.2 = (bf16[2,640,512]{1,2,0:T(8,128)(2,1)S(1)}, bf16[2,640,512]{1,2,0:T(8,128)(2,1)S(1)}, bf16[2,640]{1,0:T(2,128)(2,1)S(1)}) fusion(f32[2,640,1024]{1,2,0:T(8,128)} %copy-done.10, f32[2,640]{1,0:T(2,128)S(1)} %reshape.133, bf16[2,640,1024]{2,1,0:T(8,128)(2,1)} %bitcast.84, bf16[2,512,1024]{2,1,0:T(8,128)(2,1)} %all-gather.3.cloned.1.call-done), kind=kOutput, calls=%fused_computation.10 | convolution fusion | flops 1353317120 | bytes 12590592 | tf_op jit(solution)/shard_map/jrd,jfd->jrf/dot_general | solution.py:28
  203.4 5.6 %fusion.5 = f32[2,1024,1024]{2,1,0:T(8,128)} fusion(bf16[2,640,1024]{2,1,0:T(8,128)(2,1)S(1)} %bitcast.83, bf16[2,640,512]{1,2,0:T(8,128)(2,1)S(1)} %get-tuple-element.21, bf16[2,640,512]{1,2,0:T(8,128)(2,1)S(1)} %get-tuple-element.20), kind=kOutput, calls=%fused_computation.19 | convolution fusion | flops 2689597440 | bytes 13631488 | tf_op jit(solution)/shard_map/jrc,jrf->cjf/dot_general | solution.py:43
  209.0 9.2 %copy.96 = f32[1024,2048]{1,0:T(8,128)} copy(f32[1024,2048]{0,1:T(8,128)} %bitcast.80) | data formatting | bytes 16777216 | tf_op jit(solution)/shard_map/reshape | solution.py:44
  218.2 0.0 reduce-scatter.3.cloned.1.call-update
  218.2 1.0 copy.93
  219.2 4.8 %all-to-all-start.4 = ((bf16[1,2,640]{1,0,2:T(2,128)(2,1)}), bf16[1,2,640]{1,0,2:T(2,128)(2,1)S(1)}, u32[]{:S(2)}, u32[]{:S(2)}) async-start(bf16[1,2,640]{1,0,2:T(2,128)(2,1)} %copy.93), calls=%async_computation.4 | async-start | bytes 655360 | tf_op jit(solution)/shard_map/all_to_all | solution.py:109
  223.9 5.5 %convert_bitcast_fusion = bf16[1,2,640,1024]{3,2,1,0:T(8,128)(2,1)S(1)} fusion(bf16[2,1024,1024]{2,1,0:T(8,128)(2,1)} %all-gather.5.cloned.1.call-done, bf16[2,640,512]{1,2,0:T(8,128)(2,1)S(1)} %copy-done.9, bf16[2,640,512]{1,2,0:T(8,128)(2,1)S(1)} %copy-done.7), kind=kOutput, calls=%fused_computation.8 | convolution fusion | flops 2690908160 | bytes 9437184 | tf_op jit(solution)/shard_map/jrf,jdf->jrd/dot_general | solution.py:35
  229.4 4.3 %copy.91 = bf16[1,2,640,1024]{3,1,0,2:T(2,128)(2,1)} copy(bf16[1,2,640,1024]{3,2,1,0:T(8,128)(2,1)S(1)} %convert_bitcast_fusion) | data formatting | bytes 5242880 | tf_op jit(solution)/shard_map/broadcast_in_dim | solution.py:108
  233.7 2.6 all-to-all-done.4
  236.3 4.6 %all-to-all-start.3 = ((bf16[1,2,640,1024]{3,1,0,2:T(2,128)(2,1)}), bf16[1,2,640,1024]{3,1,0,2:T(2,128)(2,1)S(1)}, u32[]{:S(2)}, u32[]{:S(2)}) async-start(bf16[1,2,640,1024]{3,1,0,2:T(2,128)(2,1)} %copy.91), calls=%async_computation.3 | async-start | bytes 5242880 | tf_op jit(solution)/shard_map/all_to_all | solution.py:108
  240.9 0.1 copy.94
  241.0 0.1 all_to_all.62
  241.2 0.1 reshape.127
  241.3 6.8 %gather_fusion.1 = bf16[1024]{0:T(1024)(128)(2,1)S(1)} fusion(bf16[1280]{0:T(1024)(128)(2,1)S(1)} %reshape.127, s32[1024]{0:T(1024)S(1)} %broadcast_clamp_fusion), kind=kCustom, calls=%fused_computation.1 | custom fusion | bytes 8192 | tf_op jit(solution)/shard_map/gather | solution.py:115
  248.1 0.1 reshape.128
  248.2 0.7 copy.100
  248.8 52.6 %all-to-all-done.3 = bf16[1,2,640,1024]{3,1,0,2:T(2,128)(2,1)S(1)} async-done(((bf16[1,2,640,1024]{3,1,0,2:T(2,128)(2,1)}), bf16[1,2,640,1024]{3,1,0,2:T(2,128)(2,1)S(1)}, u32[]{:S(2)}, u32[]{:S(2)}) %all-to-all-start.3) | async-done | bytes 2621472 | tf_op jit(solution)/shard_map/all_to_all | solution.py:108
  301.5 1.6 copy-done.2
  303.0 2.6 copy.92
  305.6 5.4 %gather_fusion = bf16[1024,1024]{1,0:T(8,128)(2,1)} fusion(bf16[1280,1024]{1,0:T(8,128)(2,1)S(1)} %bitcast.75, s32[1024]{0:T(1024)S(1)} %broadcast_clamp_fusion), kind=kCustom, calls=%fused_computation | custom fusion | bytes 4198400 | tf_op jit(solution)/shard_map/gather | solution.py:111
  311.0 3.8 bitcast_reduce_fusion
  314.8 1.2 reshape.132
  316.0 0.8 copy.102
  316.7 54.5 %reduce-scatter.3.cloned.1.call-done = f32[64,2048]{1,0:T(8,128)} async-done(((f32[1024,2048]{1,0:T(8,128)}), f32[64,2048]{1,0:T(8,128)}) %reduce-scatter.3.cloned.1.call-update) | async-done | bytes 524304 | tf_op jit(solution)/shard_map/reduce_scatter | solution.py:93
  371.3 1.5 reshape.130
  372.7 1.0 copy.101
  (31 shorter events, 0.2 us)
Async XLA Ops:
  7.2 29.9 %copy-start = (bf16[128,1024]{1,0:T(8,128)(2,1)S(1)}, bf16[128,1024]{1,0:T(8,128)(2,1)}, u32[]{:S(2)}) copy-start(bf16[128,1024]{1,0:T(8,128)(2,1)} %param.6) | copy-start | bytes 786436
  7.2 173.9 %all-gather.5.cloned.1.call-start = ((), (), s32[]{:S(2)}) async-start(), calls=%async_computation.8 | async-start | bytes 4456448 | tf_op jit(solution)/shard_map/all_gather | solution.py:87
  28.5 16.1 %all-to-all-start = ((bf16[16,2,40]{2,1,0:T(2,128)(2,1)}), bf16[16,2,40]{2,1,0:T(2,128)(2,1)S(1)}, u32[]{:S(2)}, u32[]{:S(2)}) async-start(bf16[16,2,40]{2,1,0:T(2,128)(2,1)} %reshape.120), calls=%async_computation | async-start | bytes 16384 | tf_op jit(solution)/shard_map/all_to_all | solution.py:73
  44.6 7.0 %copy-start.5 = (bf16[128,1024]{1,0:T(8,128)(2,1)S(1)}, bf16[128,1024]{1,0:T(8,128)(2,1)}, u32[]{:S(2)}) copy-start(bf16[128,1024]{1,0:T(8,128)(2,1)} %param.7) | copy-start | bytes 786436
  44.6 67.5 %all-to-all-start.2 = ((bf16[16,2,40,1024]{3,2,1,0:T(8,128)(2,1)}), bf16[16,2,40,1024]{3,2,1,0:T(8,128)(2,1)S(1)}, u32[]{:S(2)}, u32[]{:S(2)}) async-start(bf16[16,2,40,1024]{3,2,1,0:T(8,128)(2,1)} %bitcast.79), calls=%async_computation.2 | async-start | bytes 5242880 | tf_op jit(solution)/shard_map/all_to_all | solution.py:67
  112.2 65.3 %all-to-all-start.1 = ((bf16[16,2,40,1024]{3,2,1,0:T(8,128)(2,1)}), bf16[16,2,40,1024]{3,2,1,0:T(8,128)(2,1)}, u32[]{:S(2)}, u32[]{:S(2)}) async-start(bf16[16,2,40,1024]{3,2,1,0:T(8,128)(2,1)} %bitcast.77), calls=%async_computation.1 | async-start | bytes 5242880 | tf_op jit(solution)/shard_map/all_to_all | solution.py:70
  116.8 79.9 %all-gather.3.cloned.1.call-start = ((), (), s32[]{:S(2)}) async-start(), calls=%async_computation.7 | async-start | bytes 2228224 | tf_op jit(solution)/shard_map/all_gather | solution.py:88
  117.6 197.2 %reduce-scatter.5.cloned.1.call-start = ((), (), s32[]{:S(2)}) async-start(), calls=%async_computation.10 | async-start | bytes 4456448 | tf_op jit(solution)/shard_map/reduce_scatter | solution.py:99
  177.4 3.7 copy-start.3
  181.1 5.6 %copy-start.4 = (bf16[1,2,16,40,1024]{4,3,2,1,0:T(8,128)(2,1)S(1)}, bf16[1,2,16,40,1024]{4,3,2,1,0:T(8,128)(2,1)}, u32[]{:S(2)}) copy-start(bf16[1,2,16,40,1024]{4,3,2,1,0:T(8,128)(2,1)} %copy.86) | copy-start | bytes 7864324
  186.7 4.5 %copy-start.10 = (f32[2,640,1024]{1,2,0:T(8,128)}, f32[2,640,1024]{1,2,0:T(8,128)S(1)}, u32[]{:S(2)}) copy-start(f32[2,640,1024]{1,2,0:T(8,128)S(1)} %fusion.21) | copy-start | bytes 15728644
  196.6 174.7 %reduce-scatter.3.cloned.1.call-start = ((), (), s32[]{:S(2)}) async-start(), calls=%async_computation.9 | async-start | bytes 8912896 | tf_op jit(solution)/shard_map/reduce_scatter | solution.py:93
  203.4 5.6 %copy-start.6 = (bf16[2,640,512]{1,2,0:T(8,128)(2,1)}, bf16[2,640,512]{1,2,0:T(8,128)(2,1)S(1)}, u32[]{:S(2)}) copy-start(bf16[2,640,512]{1,2,0:T(8,128)(2,1)S(1)} %get-tuple-element.20) | copy-start | bytes 3932164
  203.4 5.6 %copy-start.8 = (bf16[2,640,512]{1,2,0:T(8,128)(2,1)}, bf16[2,640,512]{1,2,0:T(8,128)(2,1)S(1)}, u32[]{:S(2)}) copy-start(bf16[2,640,512]{1,2,0:T(8,128)(2,1)S(1)} %get-tuple-element.21) | copy-start | bytes 3932164
  218.2 5.8 %copy-start.7 = (bf16[2,640,512]{1,2,0:T(8,128)(2,1)S(1)}, bf16[2,640,512]{1,2,0:T(8,128)(2,1)}, u32[]{:S(2)}) copy-start(bf16[2,640,512]{1,2,0:T(8,128)(2,1)} %copy-done.6) | copy-start | bytes 3932164
  218.2 5.8 %copy-start.9 = (bf16[2,640,512]{1,2,0:T(8,128)(2,1)S(1)}, bf16[2,640,512]{1,2,0:T(8,128)(2,1)}, u32[]{:S(2)}) copy-start(bf16[2,640,512]{1,2,0:T(8,128)(2,1)} %copy-done.8) | copy-start | bytes 3932164
  219.2 17.2 %all-to-all-start.4 = ((bf16[1,2,640]{1,0,2:T(2,128)(2,1)}), bf16[1,2,640]{1,0,2:T(2,128)(2,1)S(1)}, u32[]{:S(2)}, u32[]{:S(2)}) async-start(bf16[1,2,640]{1,0,2:T(2,128)(2,1)} %copy.93), calls=%async_computation.4 | async-start | bytes 655360 | tf_op jit(solution)/shard_map/all_to_all | solution.py:109
  236.3 65.1 %all-to-all-start.3 = ((bf16[1,2,640,1024]{3,1,0,2:T(2,128)(2,1)}), bf16[1,2,640,1024]{3,1,0,2:T(2,128)(2,1)S(1)}, u32[]{:S(2)}, u32[]{:S(2)}) async-start(bf16[1,2,640,1024]{3,1,0,2:T(2,128)(2,1)} %copy.91), calls=%async_computation.3 | async-start | bytes 5242880 | tf_op jit(solution)/shard_map/all_to_all | solution.py:108
  301.5 1.6 copy-start.2
  305.6 68.1 %copy-start.1 = (bf16[128,1024]{1,0:T(8,128)(2,1)S(1)}, bf16[128,1024]{1,0:T(8,128)(2,1)}, u32[]{:S(2)}) copy-start(bf16[128,1024]{1,0:T(8,128)(2,1)} %param.6) | copy-start | bytes 786436
Sparse Core Ops, SparseCore 0:
  10.5 59.2 all-gather.4
  120.1 50.8 all-gather.2
  196.7 81.0 reduce-scatter.4
  281.8 89.3 reduce-scatter.2
where the time goes:
time: 381 us; the launch traced here: 380 us
  waiting for transfers between devices  223 us (59%)
  local copies, waits for them, and re-layouts  72.2 us (19%)
  starting transfers between devices  29.7 us (8%)
  matrix products  27.8 us (7%)
  between operations  14.1 us (4%)
  other arithmetic  13.7 us (4%)
    all_to_all x1, waiting for transfers between devices, body(): lax.all_to_all(send_dy.reshape(block_shape), 'expert', split_axis=0, conc...  57.9 us
    reduce_scatter x1, waiting for transfers between devices, body(): lax.psum_scatter(row_terms(routed_x, pre_grad, rows_in * lax.axis_size('d...  54.5 us
    all_to_all x1, waiting for transfers between devices, body(): lax.all_to_all(send_x.reshape(block_shape), 'expert', split_axis=0, conca...  53.4 us
    all_to_all x1, waiting for transfers between devices, body(): lax.all_to_all(slot_dx[None], 'expert', split_axis=2, concat_axis=0, tile...  52.6 us
    reshape x2, local copies, waits for them, and re-layouts, row_terms(): return summed.reshape(row_count, -1)  14.6 us
    dot_general x2, matrix products, row_terms(): jnp.einsum('jrc,jrf->cjf', left_side, right_side, preferred_element_type=...  10 us
    another operation x3, other arithmetic  9.15 us
    all_to_all x1, starting transfers between devices, body(): lax.all_to_all(send_gate.reshape(owners, EXP_DEV, capacity), 'expert', sp...  8.57 us
  transfers between devices with their start and end apart: 9, of which 6 were waited for; matrix products, arithmetic and copies ran while one was open for 29% of the time, Pallas kernels for 0%

commit v1 on v0

v1 whole, which is shorter than its diff:
```python
import functools

import jax
import jax.numpy as jnp
from jax import lax
from jax.experimental import pallas as pl
from jax.experimental.pallas import tpu as pltpu
from jax.sharding import Mesh
from jax.sharding import PartitionSpec as P

BF16 = jnp.bfloat16
F32 = jnp.float32
TOP = 8
CAP = 40
TOK = 128
WIDTH = 1024
HID = 512
ROWS_IN = 64
ROWS_OUT = 32
ROWS = ROWS_IN + ROWS_OUT
CHIPS = 8
PAIR = 2 * CAP
SLOTS = CHIPS * PAIR
VMEM_LIMIT = 60 * 1024 * 1024

UP = [(i, (i + 1) % 4) for i in range(4)]
DOWN = [(i, (i - 1) % 4) for i in range(4)]


def dot(a, b, dims):
    return lax.dot_general(a, b, (dims, ((), ())), preferred_element_type=F32)


NN = ((1,), (0,))
NT = ((1,), (1,))
TN = ((0,), (0,))


def route_kernel(first_ref, pay_ref, x_ref, dy_ref, gate_ref, sel_ref):
    first = first_ref[0]
    upper = (
        lax.broadcasted_iota(jnp.int32, (TOK, TOK), 0)
        < lax.broadcasted_iota(jnp.int32, (TOK, TOK), 1)
    ).astype(BF16)
    named, weights = [], []
    for e in range(2):
        expert = (first + e).astype(F32)
        for c in range(2):
            ids = pay_ref[c, 2 * TOK : 2 * TOK + TOP, 0:TOK].astype(F32)
            probs = pay_ref[c, 2 * TOK : 2 * TOK + TOP, TOK : 2 * TOK].astype(F32)
            hit = jnp.where(ids == expert, 1.0, 0.0)
            named.append(jnp.sum(hit, axis=0, keepdims=True))
            weights.append(jnp.sum(hit * probs, axis=0, keepdims=True))
    marks = jnp.concatenate(named + named, axis=0)
    ranks = dot(marks.astype(BF16), upper, NN)
    slot = lax.broadcasted_iota(jnp.int32, (PAIR, TOK), 0).astype(F32)
    picks = []
    for e in range(2):
        halves = []
        for c in range(2):
            i = 2 * e + c
            place = jnp.where(marks[i : i + 1] > 0.5, ranks[i : i + 1] + float(CAP * c), -1.0)
            halves.append(jnp.where(slot == place, 1.0, 0.0))
        pick = jnp.concatenate(halves, axis=1)
        prob = jnp.concatenate([weights[2 * e], weights[2 * e + 1]], axis=1)
        column = jnp.sum(pick * prob, axis=1, keepdims=True)
        gate_ref[e] = jnp.broadcast_to(column, (PAIR, TOK))
        picks.append(pick)
    sel = jnp.concatenate(picks, axis=0).astype(BF16)
    sel_ref[0] = sel
    x = jnp.concatenate([pay_ref[0, 0:TOK], pay_ref[1, 0:TOK]], axis=0)
    routed = dot(sel, x, NN).astype(BF16)
    x_ref[0] = routed[:PAIR]
    x_ref[1] = routed[PAIR:]
    dy = jnp.concatenate([pay_ref[0, TOK : 2 * TOK], pay_ref[1, TOK : 2 * TOK]], axis=0)
    routed = dot(sel, dy, NN).astype(BF16)
    dy_ref[0] = routed[:PAIR]
    dy_ref[1] = routed[PAIR:]


def route(first, pay):
    return pl.pallas_call(
        route_kernel,
        name="route",
        grid_spec=pltpu.PrefetchScalarGridSpec(
            num_scalar_prefetch=1,
            grid=(CHIPS,),
            in_specs=[pl.BlockSpec((2, 2 * TOK + TOP, WIDTH), lambda p, f: (p, 0, 0))],
            out_specs=[
                pl.BlockSpec((2, PAIR, WIDTH), lambda p, f: (0, p, 0)),
                pl.BlockSpec((2, PAIR, WIDTH), lambda p, f: (0, p, 0)),
                pl.BlockSpec((2, PAIR, TOK), lambda p, f: (0, p, 0)),
                pl.BlockSpec((1, 2 * PAIR, 2 * TOK), lambda p, f: (p, 0, 0)),
            ],
        ),
        out_shape=[
            jax.ShapeDtypeStruct((2, SLOTS, WIDTH), BF16),
            jax.ShapeDtypeStruct((2, SLOTS, WIDTH), BF16),
            jax.ShapeDtypeStruct((2, SLOTS, TOK), F32),
            jax.ShapeDtypeStruct((CHIPS, 2 * PAIR, 2 * TOK), BF16),
        ],
        compiler_params=pltpu.CompilerParams(vmem_limit_bytes=VMEM_LIMIT),
        cost_estimate=pl.CostEstimate(
            flops=4 * 1024 * 1280 * 1024, bytes_accessed=14_000_000, transcendentals=0
        ),
    )(first, pay)


def expert_kernel(
    inner_first,
    place_ref,
    x_ref,
    dy_ref,
    gate_ref,
    own_ref,
    from_down_ref,
    from_up_ref,
    far_a_ref,
    far_b_ref,
    g_far_a,
    g_far_b,
    g_up,
    g_dn,
    g_own,
    dx_ref,
    sg_ref,
    w_in,
    w_out,
    pre,
    act,
    xt,
    at,
    grads,
    wsem,
    gsem,
):
    my_outer = place_ref[0]
    my_inner = place_ref[1]

    def block_of(outer, inner):
        return inner * 4 + outer if inner_first else outer * 4 + inner

    loads = []
    n = 0
    for oj in range(4):
        for ij in range(4):
            if oj == 0:
                src = own_ref.at[ij]
            elif oj == 1:
                src = from_down_ref.at[ij]
            elif oj == 3:
                src = from_up_ref.at[ij]
            elif ij < 2:
                src = far_a_ref.at[ij]
            else:
                src = far_b_ref.at[ij - 2]
            outer = lax.rem(my_outer + 4 - oj, 4)
            inner = lax.rem(my_inner + 4 - ij, 4)
            b = block_of(outer, inner)
            for part, dst in ((pl.ds(0, ROWS_IN), w_in), (pl.ds(ROWS_IN, ROWS_OUT), w_out)):
                copy = pltpu.make_async_copy(src.at[part, :], dst.at[b], wsem.at[n])
                copy.start()
                loads.append(copy)
                n += 1

    def flip(i, _):
        c = pl.multiple_of(i * 128, 128)
        xt[pl.ds(c, 128), :] = x_ref[0, :, pl.ds(c, 128)].T
        return 0

    lax.fori_loop(0, WIDTH // 128, flip, 0)
    for copy in loads:
        copy.wait()

    x = x_ref.at[0]
    dy = dy_ref.at[0]
    tile = 256
    sg_ref[...] = jnp.zeros_like(sg_ref)

    def forward(i, _):
        lo = pl.multiple_of(i * tile, tile)
        hi = pl.multiple_of(HID + i * tile, tile)
        wg = w_in[:, :, pl.ds(lo, tile)].reshape(WIDTH, tile)
        wu = w_in[:, :, pl.ds(hi, tile)].reshape(WIDTH, tile)
        wd = w_out[pl.ds(i * (tile // ROWS_OUT), tile // ROWS_OUT)].reshape(tile, WIDTH)
        gate_pre = dot(x[...], wg, NN)
        up_pre = dot(x[...], wu, NN)
        raw = dot(dy[...], wd, NT)
        prob = gate_ref[0, :, 0:1]
        s = jax.nn.sigmoid(gate_pre)
        silu = gate_pre * s
        activation = silu * up_pre
        act_grad = prob * raw
        d_gate = act_grad * up_pre * s * (1.0 + gate_pre * (1.0 - s))
        pre[:, pl.ds(lo, tile)] = d_gate.astype(BF16)
        pre[:, pl.ds(hi, tile)] = (act_grad * silu).astype(BF16)
        act[:, pl.ds(lo, tile)] = (prob * activation).astype(BF16)
        total = jnp.sum(activation * raw, axis=1, keepdims=True)
        sg_ref[...] += jnp.broadcast_to(total, sg_ref.shape)
        return 0

    lax.fori_loop(0, HID // tile, forward, 0)

    def flip_act(i, _):
        c = pl.multiple_of(i * 128, 128)
        at[pl.ds(c, 128), :] = act[:, pl.ds(c, 128)].T
        return 0

    lax.fori_loop(0, HID // 128, flip_act, 0)

    def backward(i, _):
        lo = pl.multiple_of(i * tile, tile)
        g_in = dot(xt[...], pre[:, pl.ds(lo, tile)], NN).astype(BF16)
        g_out = dot(at[...], dy[:, pl.ds(lo, tile)], NN).astype(BF16)
        for outer in range(4):
            for inner in range(4):
                b = block_of(outer, inner)
                oj = lax.rem(outer + 4 - my_outer, 4)
                ij = lax.rem(inner + 4 - my_inner, 4)
                grads[oj, ij, 0:ROWS_IN, pl.ds(lo, tile)] = g_in[b * ROWS_IN : (b + 1) * ROWS_IN]
                grads[oj, ij, ROWS_IN:ROWS, pl.ds(lo, tile)] = g_out[
                    b * ROWS_OUT : (b + 1) * ROWS_OUT
                ]
        return 0

    lax.fori_loop(0, WIDTH // tile, backward, 0)
    stores = [
        pltpu.make_async_copy(grads.at[2, pl.ds(0, 2)], g_far_a, gsem.at[0]),
        pltpu.make_async_copy(grads.at[2, pl.ds(2, 2)], g_far_b, gsem.at[1]),
        pltpu.make_async_copy(grads.at[1], g_up, gsem.at[2]),
        pltpu.make_async_copy(grads.at[3], g_dn, gsem.at[3]),
        pltpu.make_async_copy(grads.at[0], g_own, gsem.at[4]),
    ]
    for copy in stores:
        copy.start()

    def input_grad(i, _):
        b = i * (tile // ROWS_IN)
        w = w_in[pl.ds(b, tile // ROWS_IN)].reshape(tile, WIDTH)
        lo = pl.multiple_of(i * tile, tile)
        dx_ref[:, pl.ds(lo, tile)] = dot(pre[...], w, NT).astype(BF16)
        return 0

    lax.fori_loop(0, WIDTH // tile, input_grad, 0)
    for copy in stores:
        copy.wait()


def expert(e, inner_first, place, x, dy, gate, pieces):
    any_spec = pl.BlockSpec(memory_space=pl.ANY)
    return pl.pallas_call(
        functools.partial(expert_kernel, inner_first),
        name="expert",
        grid_spec=pltpu.PrefetchScalarGridSpec(
            num_scalar_prefetch=1,
            grid=(1,),
            in_specs=[
                pl.BlockSpec((1, SLOTS, WIDTH), lambda i, f: (e, 0, 0)),
                pl.BlockSpec((1, SLOTS, WIDTH), lambda i, f: (e, 0, 0)),
                pl.BlockSpec((1, SLOTS, TOK), lambda i, f: (e, 0, 0)),
            ]
            + [any_spec] * 5,
            out_specs=[any_spec] * 5
            + [
                pl.BlockSpec((SLOTS, WIDTH), lambda i, f: (0, 0)),
                pl.BlockSpec((SLOTS, TOK), lambda i, f: (0, 0)),
            ],
            scratch_shapes=[
                pltpu.VMEM((16, ROWS_IN, WIDTH), BF16),
                pltpu.VMEM((16, ROWS_OUT, WIDTH), BF16),
                pltpu.VMEM((SLOTS, WIDTH), BF16),
                pltpu.VMEM((SLOTS, HID), BF16),
                pltpu.VMEM((WIDTH, SLOTS), BF16),
                pltpu.VMEM((HID, SLOTS), BF16),
                pltpu.VMEM((4, 4, ROWS, WIDTH), BF16),
                pltpu.SemaphoreType.DMA((32,)),
                pltpu.SemaphoreType.DMA((5,)),
            ],
        ),
        out_shape=[
            jax.ShapeDtypeStruct((2, ROWS, WIDTH), BF16),
            jax.ShapeDtypeStruct((2, ROWS, WIDTH), BF16),
            jax.ShapeDtypeStruct((4, ROWS, WIDTH), BF16),
            jax.ShapeDtypeStruct((4, ROWS, WIDTH), BF16),
            jax.ShapeDtypeStruct((4, ROWS, WIDTH), BF16),
            jax.ShapeDtypeStruct((SLOTS, WIDTH), BF16),
            jax.ShapeDtypeStruct((SLOTS, TOK), F32),
        ],
        compiler_params=pltpu.CompilerParams(vmem_limit_bytes=VMEM_LIMIT),
        cost_estimate=pl.CostEstimate(
            flops=2 * 640 * 1024 * 4096, bytes_accessed=12_000_000, transcendentals=640 * 512
        ),
    )(place, x, dy, gate, *pieces)


def combine_kernel(first_ref, meta_ref, sel_ref, dx0_ref, dx1_ref, sg0_ref, sg1_ref, out_ref):
    first = first_ref[0]
    sel = sel_ref[0]
    rows = jnp.concatenate([dx0_ref[...], dx1_ref[...]], axis=0)
    back = dot(sel, rows, TN).astype(BF16)
    sums = jnp.concatenate([sg0_ref[:, 0:1], sg1_ref[:, 0:1]], axis=0)
    sums = sums.astype(BF16).astype(F32)
    spread = sel.astype(F32) * sums
    totals = [
        jnp.sum(spread[:PAIR], axis=0, keepdims=True),
        jnp.sum(spread[PAIR:], axis=0, keepdims=True),
    ]
    for c in range(2):
        out_ref[c, 0, 0:TOK] = back[c * TOK : (c + 1) * TOK]
        ids = meta_ref[c, :, 0:TOK].astype(F32)
        value = jnp.zeros((TOP, TOK), F32)
        for e in range(2):
            hit = ids == (first + e).astype(F32)
            value = value + jnp.where(hit, totals[e][:, c * TOK : (c + 1) * TOK], 0.0)
        out_ref[c, 0, TOK : TOK + TOP] = jnp.zeros((TOP, WIDTH), BF16)
        out_ref[c, 0, TOK : TOK + TOP, 0:TOK] = value.astype(BF16)


def combine(first, pay, sel, dx0, dx1, sg0, sg1):
    return pl.pallas_call(
        combine_kernel,
        name="combine",
        grid_spec=pltpu.PrefetchScalarGridSpec(
            num_scalar_prefetch=1,
            grid=(CHIPS,),
            in_specs=[
                pl.BlockSpec((2, TOP, 2 * TOK), lambda p, f: (p, 2 * TOK // TOP, 0)),
                pl.BlockSpec((1, 2 * PAIR, 2 * TOK), lambda p, f: (p, 0, 0)),
                pl.BlockSpec((PAIR, WIDTH), lambda p, f: (p, 0)),
                pl.BlockSpec((PAIR, WIDTH), lambda p, f: (p, 0)),
                pl.BlockSpec((PAIR, TOK), lambda p, f: (p, 0)),
                pl.BlockSpec((PAIR, TOK), lambda p, f: (p, 0)),
            ],
            out_specs=pl.BlockSpec((2, 1, TOK + TOP, WIDTH), lambda p, f: (0, p, 0, 0)),
        ),
        out_shape=jax.ShapeDtypeStruct((2, CHIPS, TOK + TOP, WIDTH), BF16),
        compiler_params=pltpu.CompilerParams(vmem_limit_bytes=VMEM_LIMIT),
        cost_estimate=pl.CostEstimate(
            flops=2 * 1280 * 256 * 1024, bytes_accessed=8_000_000, transcendentals=0
        ),
    )(first, pay, sel, dx0, dx1, sg0, sg1)


def gather_ring(block, axis):
    half = block.shape[0] // 2
    below = lax.ppermute(block, axis, UP)
    above = lax.ppermute(block, axis, DOWN)
    far_a = lax.ppermute(below[:half], axis, UP)
    far_b = lax.ppermute(above[half:], axis, DOWN)
    return block, below, above, far_a, far_b


def gather_weights(own, inner, outer):
    own, below, above, far_a, far_b = gather_ring(own, inner)
    far = jnp.concatenate([far_a, far_b], axis=0)
    row = jnp.stack([own, below, far, above], axis=0)
    return gather_ring(row, outer)


def add(a, b):
    return a.astype(F32) + b.astype(F32)


def reduce_ring(far_a, far_b, up, down, own, axis):
    half = far_a.shape[0]
    from_below = lax.ppermute(far_a, axis, UP)
    from_above = lax.ppermute(far_b, axis, DOWN)
    up = jnp.concatenate([add(up[:half], from_below).astype(BF16), up[half:]], axis=0)
    down = jnp.concatenate([down[:half], add(down[half:], from_above).astype(BF16)], axis=0)
    from_below = lax.ppermute(up, axis, UP)
    from_above = lax.ppermute(down, axis, DOWN)
    return add(own, from_below) + from_above.astype(F32)


def reduce_grads(pieces, outer, inner):
    total = reduce_ring(*pieces, outer)
    rounded = total.astype(BF16)
    half = ROWS // 2
    return reduce_ring(
        rounded[2, :half], rounded[2, half:], rounded[1], rounded[3], total[0], inner
    )


def body(tokens, cotangent, expert_ids, gate_probs, gate_up, down_proj):
    ix, iy = lax.axis_index("x"), lax.axis_index("y")
    first = (2 * (2 * lax.axis_index("z") + lax.axis_index("core"))).astype(jnp.int32)[None]
    meta = jnp.concatenate(
        [
            expert_ids.T.astype(BF16),
            gate_probs.T,
            jnp.zeros((TOP, WIDTH - 2 * TOK), BF16),
        ],
        axis=1,
    )
    pay = jnp.concatenate([tokens, cotangent, meta], axis=0)
    pay = lax.all_gather(pay, ("z", "core"), axis=0, tiled=False)
    own = jnp.concatenate([gate_up, down_proj], axis=1)
    pieces0 = gather_weights(own[0], "x", "y")
    pieces1 = gather_weights(own[1], "y", "x")
    place0 = jnp.stack([iy, ix]).astype(jnp.int32)
    place1 = jnp.stack([ix, iy]).astype(jnp.int32)

    x, dy, gate, sel = route(first, pay)
    *g0, dx0, sg0 = expert(0, False, place0, x, dy, gate, pieces0)
    *g1, dx1, sg1 = expert(1, True, place1, x, dy, gate, pieces1)
    total0 = reduce_grads(g0, "y", "x")
    total1 = reduce_grads(g1, "x", "y")

    part = combine(first, pay, sel, dx0, dx1, sg0, sg1)
    pair = lax.all_to_all(part, "core", split_axis=0, concat_axis=0, tiled=True)
    pair = add(pair[0], pair[1]).astype(BF16).reshape(CHIPS * (TOK + TOP), WIDTH)
    done = lax.psum_scatter(pair, "z", scatter_dimension=0, tiled=True)
    grad_tokens = done[:TOK]
    grad_gates = done[TOK:, :TOK].T
    grad_gate_up = jnp.stack([total0[:ROWS_IN], total1[:ROWS_IN]], axis=0)
    grad_down = jnp.stack([total0[ROWS_IN:], total1[ROWS_IN:]], axis=0)
    return grad_tokens, grad_gates, grad_gate_up, grad_down


def solution(mesh):
    grid = Mesh(mesh.devices.reshape(4, 4, 8, 2), ("y", "x", "z", "core"))
    rows = P(("y", "x", "z", "core"), None)
    held = P(("z", "core"), ("y", "x"), None)
    return jax.shard_map(
        body,
        mesh=grid,
        in_specs=(rows, rows, rows, rows, held, held),
        out_specs=(rows, rows, held, held),
        check_vma=False,
    )
```

time: 381 us -> 192 us (0.50)
  waiting for transfers between devices: 223 us -> 52.6 us
  local copies, waits for them, and re-layouts: 72.2 us -> 7.66 us
  Pallas kernels: 0 us -> 47.1 us
  matrix products: 27.8 us -> 0 us
  starting transfers between devices: 29.7 us -> 47.5 us
  blocking collectives: 0 us -> 8.71 us
    all_to_all x5 -> x0, waiting for transfers between devices: 167 us -> none  [the longest x1 57.9 us: body(): lax.all_to_all(send_dy.reshape(block_shape), 'expert', split_axis=0, conc...]
    reduce_scatter x2 -> x1, waiting for transfers between devices: 54.5 us -> 0.01 us  [body(): done = lax.psum_scatter(pair, 'z', scatter_dimension=0, tiled=True)]
    ppermute x0 -> x32, starting transfers between devices: none -> 47.5 us  [the longest x4 7.68 us: gather_ring(): above = lax.ppermute(block, axis, DOWN)]
    pallas_call x0 -> x4, Pallas kernels: none -> 47.1 us  [the longest x2 29.3 us: expert(): pl.pallas_call(functools.partial(expert_kernel, inner_first), name='exper...]
    ppermute x0 -> x32, waiting for transfers between devices: none -> 35.5 us  [the longest x4 14.9 us: reduce_ring(): from_below = lax.ppermute(up, axis, UP)]
    all_to_all x5 -> x0, starting transfers between devices: 29.5 us -> none  [the longest x1 8.57 us: body(): lax.all_to_all(send_gate.reshape(owners, EXP_DEV, capacity), 'expert', sp...]
    dot_general x5 -> x0, matrix products: 27.8 us -> none  [the longest x2 10 us: row_terms(): jnp.einsum('jrc,jrf->cjf', left_side, right_side, preferred_element_type=...]
    scatter x3 -> x0, local copies, waits for them, and re-layouts: 21.8 us -> none  [the longest x1 7.59 us: body(): jnp.zeros((buffer_rows,), jnp.bfloat16).at[slot_dest]]
  transfers between devices with their start and end apart: 9 -> 34, of which waited for: 6 -> 10; matrix products, arithmetic and copies ran while one was open for 29% -> 7% of each run, Pallas kernels for 0% -> 25%
where the time goes in v1:
time: 192 us; the launch traced here: 191 us
  waiting for transfers between devices  52.6 us (27%)
  starting transfers between devices  47.5 us (25%)
  Pallas kernels  47.1 us (25%)
  between operations  14.5 us (8%)
  other arithmetic  13.3 us (7%)
  blocking collectives  8.71 us (5%)
  local copies, waits for them, and re-layouts  7.66 us (4%)
    pallas_call x2, Pallas kernels, expert(): pl.pallas_call(functools.partial(expert_kernel, inner_first), name='exper...  29.3 us
    all_gather x1, waiting for transfers between devices, body(): pay = lax.all_gather(pay, ('z', 'core'), axis=0, tiled=False)  17.2 us
    ppermute x4, waiting for transfers between devices, reduce_ring(): from_below = lax.ppermute(up, axis, UP)  14.9 us
    ppermute x4, waiting for transfers between devices, gather_ring(): below = lax.ppermute(block, axis, UP)  12.1 us
    pallas_call x1, Pallas kernels, route(): pl.pallas_call(route_kernel, name='route', grid_spec=pltpu.PrefetchScalar...  9.99 us
    all_to_all x1, blocking collectives, body(): pair = lax.all_to_all(part, 'core', split_axis=0, concat_axis=0, tiled=True)  8.71 us
    pallas_call x1, Pallas kernels, combine(): pl.pallas_call(combine_kernel, name='combine', grid_spec=pltpu.PrefetchSc...  7.77 us
    ppermute x4, starting transfers between devices, gather_ring(): above = lax.ppermute(block, axis, DOWN)  7.68 us
  transfers between devices with their start and end apart: 34, of which 10 were waited for; matrix products, arithmetic and copies ran while one was open for 7% of the time, Pallas kernels for 25%

profile of v1, /device:TPU:24, one launch (start us, length us, event | category | flops | bytes accessed | tf_op | source)
XLA Modules:
  0.0 191.5 jit_solution(11158847544678050006)
XLA Ops:
  7.2 0.7 convert_bitcast_fusion
  8.0 1.9 maximum_maximum_fusion
  10.1 1.6 collective-permute-start
  11.6 1.7 collective-permute-start.2
  13.4 0.7 collective-permute-start.10
  14.1 2.5 %collective-permute-start.8 = (bf16[96,1024]{1,0:T(8,128)(2,1)S(1)}, bf16[96,1024]{1,0:T(8,128)(2,1)S(1)}, u32[]{:S(2)}, u32[]{:S(2)}) collective-permute-start(bf16[96,1024]{1,0:T(8,128)(2,1)S(1)} %get-tuple-element.58), channel_id=1, source_target_pairs={{0,64},{64,128},{128,192},{192,0},{1,65},{65,129},{129,193},{193,1... | collective-permute-start | bytes 589832 | tf_op jit(solution)/shard_map/ppermute | solution.py:346
  16.6 1.4 collective-permute-done
  18.0 0.4 collective-permute-start.1
  18.4 3.0 %collective-permute-start.3 = (bf16[48,1024]{1,0:T(8,128)(2,1)S(1)}, bf16[48,1024]{1,0:T(8,128)(2,1)S(1)}, u32[]{:S(2)}, u32[]{:S(2)}) collective-permute-start(bf16[48,1024]{1,0:T(8,128)(2,1)S(1)} %slice.194), channel_id=1, source_target_pairs={{0,48},{16,0},{32,16},{48,32},{1,49},{17,1},{33,17},{49,33},{2,50}... | collective-permute-start | bytes 294920 | tf_op jit(solution)/shard_map/ppermute | solution.py:349
  21.4 0.8 collective-permute-start.11
  22.3 2.6 %collective-permute-start.9 = (bf16[48,1024]{1,0:T(8,128)(2,1)S(1)}, bf16[48,1024]{1,0:T(8,128)(2,1)S(1)}, u32[]{:S(2)}, u32[]{:S(2)}) collective-permute-start(bf16[48,1024]{1,0:T(8,128)(2,1)S(1)} %slice.198), channel_id=1, source_target_pairs={{0,64},{64,128},{128,192},{192,0},{1,65},{65,129},{129,193},{193,1... | collective-permute-start | bytes 294920 | tf_op jit(solution)/shard_map/ppermute | solution.py:348
  25.0 0.1 collective-permute-start.4
  25.1 2.0 %collective-permute-start.5 = (bf16[4,96,1024]{2,1,0:T(8,128)(2,1)S(1)}, bf16[4,96,1024]{2,1,0:T(8,128)(2,1)}, u32[]{:S(2)}, u32[]{:S(2)}) collective-permute-start(bf16[4,96,1024]{2,1,0:T(8,128)(2,1)S(1)} %pad_maximum_fusion.own_ref), channel_id=1, source_target_pairs={{0,192},{64,0},{128,64},{192,128},{1,193},{65,1},{129,65},{193,129... | collective-permute-start | bytes 2359304 | tf_op jit(solution)/shard_map/ppermute | solution.py:347
  27.1 0.9 collective-permute-done.11
  27.9 0.1 collective-permute-done.9
  28.3 3.2 %collective-permute-start.13 = (bf16[4,96,1024]{2,1,0:T(8,128)(2,1)S(1)}, bf16[4,96,1024]{2,1,0:T(8,128)(2,1)}, u32[]{:S(2)}, u32[]{:S(2)}) collective-permute-start(bf16[4,96,1024]{2,1,0:T(8,128)(2,1)S(1)} %pad_maximum_fusion.1.own_ref), channel_id=1, source_target_pairs={{0,48},{16,0},{32,16},{48,32},{1,49},{17,1},{33,17},{49,33},{2,50}... | collective-permute-start | bytes 2359304 | tf_op jit(solution)/shard_map/ppermute | solution.py:347
  31.5 0.7 pad_add_fusion.place_ref
  32.2 0.6 pad_add_fusion.1.place_ref
  32.8 10.7 %collective-permute-done.4.from_down_ref = bf16[4,96,1024]{2,1,0:T(8,128)(2,1)} collective-permute-done((bf16[4,96,1024]{2,1,0:T(8,128)(2,1)S(1)}, bf16[4,96,1024]{2,1,0:T(8,128)(2,1)}, u32[]{:S(2)}, u32[]{:S(2)}) %collective-permute-start.4) | collective-permute-done | bytes 786464 | tf_op jit(solution)/shard_map/ppermute | solution.py:346
  43.5 1.0 slice.195
  44.5 2.4 %collective-permute-start.6 = (bf16[2,96,1024]{2,1,0:T(8,128)(2,1)S(1)}, bf16[2,96,1024]{2,1,0:T(8,128)(2,1)}, u32[]{:S(2)}, u32[]{:S(2)}) collective-permute-start(bf16[2,96,1024]{2,1,0:T(8,128)(2,1)S(1)} %slice.195), channel_id=1, source_target_pairs={{0,64},{64,128},{128,192},{192,0},{1,65},{65,129},{129,193},{193,1... | collective-permute-start | bytes 1179656 | tf_op jit(solution)/shard_map/ppermute | solution.py:348
  46.9 1.0 slice.196
  48.1 0.3 collective-permute-start.14
  48.4 1.0 slice.201
  49.4 3.3 %collective-permute-start.15 = (bf16[2,96,1024]{2,1,0:T(8,128)(2,1)S(1)}, bf16[2,96,1024]{2,1,0:T(8,128)(2,1)}, u32[]{:S(2)}, u32[]{:S(2)}) collective-permute-start(bf16[2,96,1024]{2,1,0:T(8,128)(2,1)S(1)} %slice.201), channel_id=1, source_target_pairs={{0,48},{16,0},{32,16},{48,32},{1,49},{17,1},{33,17},{49,33},{2,50}... | collective-permute-start | bytes 1179656 | tf_op jit(solution)/shard_map/ppermute | solution.py:349
  52.7 17.2 %all-gather.3.cloned.1.call-done = bf16[4224,1024]{1,0:T(8,128)(2,1)} async-done(((bf16[264,1024]{1,0:T(8,128)(2,1)}), bf16[4224,1024]{1,0:T(8,128)(2,1)}) %all-gather.3.cloned.1.call-update) | async-done | bytes 8650768 | tf_op jit(solution)/shard_map/all_gather | solution.py:396
  69.9 10.0 %route.1 = (bf16[2,640,1024]{2,1,0:T(8,128)(2,1)}, bf16[2,640,1024]{2,1,0:T(8,128)(2,1)}, f32[2,640,128]{2,1,0:T(8,128)}, bf16[8,160,256]{2,1,0:T(8,128)(2,1)}) custom-call(s32[1]{0:T(128)} %bitcast.first_ref, bf16[16,264,1024]{2,1,0:T(8,128)(2,1)} %bitcast.79), custom_call_target="tpu_custom_call" | custom-call | flops 5368709120 | bytes 14000000 | tf_op jit(solution)/shard_map/route/pallas_call | solution.py:82
  79.9 14.7 %expert.2 = (bf16[2,96,1024]{2,1,0:T(8,128)(2,1)}, bf16[2,96,1024]{2,1,0:T(8,128)(2,1)}, bf16[4,96,1024]{2,1,0:T(8,128)(2,1)}, bf16[4,96,1024]{2,1,0:T(8,128)(2,...) custom-call(s32[2]{0:T(128)} %pad_add_fusion.place_ref, ...), custom_call_target="tpu_custom_call" | custom-call | flops 5368709120 | bytes 12000000 | tf_op jit(solution)/shard_map/expert/pallas_call | solution.py:251
  94.6 0.6 collective-permute-start.16
  95.2 1.5 collective-permute-start.18
  96.7 14.6 %expert.3 = (bf16[2,96,1024]{2,1,0:T(8,128)(2,1)}, bf16[2,96,1024]{2,1,0:T(8,128)(2,1)}, bf16[4,96,1024]{2,1,0:T(8,128)(2,1)}, bf16[4,96,1024]{2,1,0:T(8,128)(2,...) custom-call(s32[2]{0:T(128)} %pad_add_fusion.1.place_ref, ...), custom_call_target="tpu_custom_call" | custom-call | flops 5368709120 | bytes 12000000 | tf_op jit(solution)/shard_map/expert/pallas_call | solution.py:251
  111.4 1.5 collective-permute-start.24
  112.9 1.8 collective-permute-start.26
  114.7 7.8 %combine.1 = bf16[2,8,136,1024]{3,2,1,0:T(8,128)(2,1)} custom-call(s32[1]{0:T(128)} %bitcast.first_ref, bf16[16,264,1024]{2,1,0:T(8,128)(2,1)} %bitcast.80, bf16[8,160,256]{2,1,0:T(8,128)(2,1)} %get-tuple-element.22.sel_ref, bf16[640,1024]{1,0:T(8,128)(2,1)} %get-tuple-element.26.dx0_ref, bf16[640,1024]{1,0:T(8,128)(2,1)} %get-tuple-element.27.dx1_ref, ...), custom_call_target="tpu_custom_call" | custom-call | flops 671088640 | bytes 8000000 | tf_op jit(solution)/shard_map/combine/pallas_call | solution.py:320
  122.4 8.7 %all_to_all.5 = bf16[2,8,136,1024]{3,2,1,0:T(8,128)(2,1)S(1)} all-to-all(bf16[2,8,136,1024]{3,2,1,0:T(8,128)(2,1)} %combine.1), channel_id=1, replica_groups=mesh['y'=4,'x'=4,'z'=8,'core'=2] {'core'}, dimensions={0} | all-to-all | bytes 8912896 | tf_op jit(solution)/shard_map/all_to_all | solution.py:410
  131.1 2.4 %add_convert_fusion = bf16[1,8,136,1024]{3,2,1,0:T(8,128)(2,1)} fusion(bf16[2,8,136,1024]{3,2,1,0:T(8,128)(2,1)S(1)} %all_to_all.5), kind=kLoop, calls=%fused_computation | loop fusion | flops 4456448 | bytes 6684672 | tf_op jit(solution)/shard_map/convert_element_type | solution.py:411
  133.7 1.1 copy-done.7
  134.7 0.2 copy-done.5
  135.0 1.2 add_convert_fusion.4
  136.4 2.0 %collective-permute-start.17 = (bf16[4,96,1024]{2,1,0:T(8,128)(2,1)S(1)}, bf16[4,96,1024]{2,1,0:T(8,128)(2,1)S(1)}, u32[]{:S(2)}, u32[]{:S(2)}) collective-permute-start(bf16[4,96,1024]{2,1,0:T(8,128)(2,1)S(1)} %pad_maximum_fusion.2), channel_id=1, source_target_pairs={{0,64},{64,128},{128,192},{192,0},{1,65},{65,129},{129,193},{193,1... | collective-permute-start | bytes 2359304 | tf_op jit(solution)/shard_map/ppermute | solution.py:370
  138.3 0.1 add_convert_fusion.3
  138.6 0.4 collective-permute-start.19
  139.0 1.1 add_convert_fusion.2
  140.2 0.3 collective-permute-start.25
  140.5 1.1 add_convert_fusion.1
  141.8 3.1 %collective-permute-start.27 = (bf16[4,96,1024]{2,1,0:T(8,128)(2,1)S(1)}, bf16[4,96,1024]{2,1,0:T(8,128)(2,1)S(1)}, u32[]{:S(2)}, u32[]{:S(2)}) collective-permute-start(bf16[4,96,1024]{2,1,0:T(8,128)(2,1)S(1)} %pad_maximum_fusion.5), channel_id=1, source_target_pairs={{0,48},{16,0},{32,16},{48,32},{1,49},{17,1},{33,17},{49,33},{2,50}... | collective-permute-start | bytes 2359304 | tf_op jit(solution)/shard_map/ppermute | solution.py:371
  144.8 11.4 %collective-permute-done.17 = bf16[4,96,1024]{2,1,0:T(8,128)(2,1)S(1)} collective-permute-done((bf16[4,96,1024]{2,1,0:T(8,128)(2,1)S(1)}, bf16[4,96,1024]{2,1,0:T(8,128)(2,1)S(1)}, u32[]{:S(2)}, u32[]{:S(2)}) %collective-permute-start.17) | collective-permute-done | bytes 786464 | tf_op jit(solution)/shard_map/ppermute | solution.py:370
  156.2 2.9 %collective-permute-done.19 = bf16[4,96,1024]{2,1,0:T(8,128)(2,1)S(1)} collective-permute-done((bf16[4,96,1024]{2,1,0:T(8,128)(2,1)S(1)}, bf16[4,96,1024]{2,1,0:T(8,128)(2,1)S(1)}, u32[]{:S(2)}, u32[]{:S(2)}) %collective-permute-start.19) | collective-permute-done | bytes 786464 | tf_op jit(solution)/shard_map/ppermute | solution.py:371
  159.2 0.5 fusion.8
  159.7 0.3 collective-permute-start.20
  160.0 3.0 %collective-permute-start.22 = (bf16[48,1024]{1,0:T(8,128)(2,1)S(1)}, bf16[48,1024]{1,0:T(8,128)(2,1)S(1)}, u32[]{:S(2)}, u32[]{:S(2)}) collective-permute-start(bf16[48,1024]{1,0:T(8,128)(2,1)S(1)} %get-tuple-element.47), channel_id=1, source_target_pairs={{0,48},{16,0},{32,16},{48,32},{1,49},{17,1},{33,17},{49,33},{2,50}... | collective-permute-start | bytes 294920 | tf_op jit(solution)/shard_map/ppermute | solution.py:367
  163.0 0.5 fusion.9
  163.5 2.1 %collective-permute-start.28 = (bf16[48,1024]{1,0:T(8,128)(2,1)S(1)}, bf16[48,1024]{1,0:T(8,128)(2,1)S(1)}, u32[]{:S(2)}, u32[]{:S(2)}) collective-permute-start(bf16[48,1024]{1,0:T(8,128)(2,1)S(1)} %get-tuple-element.52), channel_id=1, source_target_pairs={{0,64},{64,128},{128,192},{192,0},{1,65},{65,129},{129,193},{193,1... | collective-permute-start | bytes 294920 | tf_op jit(solution)/shard_map/ppermute | solution.py:366
  165.7 1.0 collective-permute-start.21
  166.8 2.8 %collective-permute-start.23 = (bf16[96,1024]{1,0:T(8,128)(2,1)S(1)}, bf16[96,1024]{1,0:T(8,128)(2,1)S(1)}, u32[]{:S(2)}, u32[]{:S(2)}) collective-permute-start(bf16[96,1024]{1,0:T(8,128)(2,1)S(1)} %pad_maximum_fusion.9), channel_id=1, source_target_pairs={{0,48},{16,0},{32,16},{48,32},{1,49},{17,1},{33,17},{49,33},{2,50}... | collective-permute-start | bytes 589832 | tf_op jit(solution)/shard_map/ppermute | solution.py:371
  169.6 1.8 collective-permute-done.30
  171.5 1.5 collective-permute-start.29
  173.0 0.7 collective-permute-start.31
  173.9 3.4 %collective-permute-done.29 = bf16[96,1024]{1,0:T(8,128)(2,1)S(1)} collective-permute-done((bf16[96,1024]{1,0:T(8,128)(2,1)S(1)}, bf16[96,1024]{1,0:T(8,128)(2,1)S(1)}, u32[]{:S(2)}, u32[]{:S(2)}) %collective-permute-start.29) | collective-permute-done | bytes 196640 | tf_op jit(solution)/shard_map/ppermute | solution.py:370
  177.3 2.7 %collective-permute-done.31 = bf16[96,1024]{1,0:T(8,128)(2,1)S(1)} collective-permute-done((bf16[96,1024]{1,0:T(8,128)(2,1)S(1)}, bf16[96,1024]{1,0:T(8,128)(2,1)S(1)}, u32[]{:S(2)}, u32[]{:S(2)}) %collective-permute-start.31) | collective-permute-done | bytes 196640 | tf_op jit(solution)/shard_map/ppermute | solution.py:371
  180.1 0.7 pad_maximum_fusion.7
  180.9 0.8 pad_maximum_fusion.6
  181.7 1.7 slice.204
  183.4 1.3 slice_bitcast_fusion.18
  (88 shorter events, 1.6 us)
Async XLA Ops:
  7.2 2.8 %copy-start.9 = (bf16[2,64,1024]{2,1,0:T(8,128)(2,1)S(1)}, bf16[2,64,1024]{2,1,0:T(8,128)(2,1)}, u32[]{:S(2)}) copy-start(bf16[2,64,1024]{2,1,0:T(8,128)(2,1)} %param.10) | copy-start | bytes 786436
  7.2 2.8 %copy-start.11 = (bf16[2,32,1024]{2,1,0:T(8,128)(2,1)S(1)}, bf16[2,32,1024]{2,1,0:T(8,128)(2,1)}, u32[]{:S(2)}) copy-start(bf16[2,32,1024]{2,1,0:T(8,128)(2,1)} %param.11) | copy-start | bytes 393220
  7.2 62.7 %all-gather.3.cloned.1.call-start = ((), (), s32[]{:S(2)}) async-start(), calls=%async_computation.3 | async-start | bytes 9191424 | tf_op jit(solution)/shard_map/all_gather | solution.py:396
  9.9 171.8 %reduce-scatter.2.cloned.1.call-start = ((), (), s32[]{:S(2)}) async-start(), calls=%async_computation.2 | async-start | bytes 2506752 | tf_op jit(solution)/shard_map/reduce_scatter | solution.py:412
  10.1 7.9 %collective-permute-start = (bf16[96,1024]{1,0:T(8,128)(2,1)S(1)}, bf16[96,1024]{1,0:T(8,128)(2,1)S(1)}, u32[]{:S(2)}, u32[]{:S(2)}) collective-permute-start(bf16[96,1024]{1,0:T(8,128)(2,1)S(1)} %get-tuple-element.57), channel_id=1, source_target_pairs={{0,16},{16,32},{32,48},{48,0},{1,17},{17,33},{33,49},{49,1},{2,18}... | collective-permute-start | bytes 589832 | tf_op jit(solution)/shard_map/ppermute | solution.py:346
  11.6 6.7 %collective-permute-start.2 = (bf16[96,1024]{1,0:T(8,128)(2,1)S(1)}, bf16[96,1024]{1,0:T(8,128)(2,1)S(1)}, u32[]{:S(2)}, u32[]{:S(2)}) collective-permute-start(bf16[96,1024]{1,0:T(8,128)(2,1)S(1)} %get-tuple-element.57), channel_id=1, source_target_pairs={{0,48},{16,0},{32,16},{48,32},{1,49},{17,1},{33,17},{49,33},{2,50}... | collective-permute-start | bytes 589832 | tf_op jit(solution)/shard_map/ppermute | solution.py:347
  13.4 8.0 %collective-permute-start.10 = (bf16[96,1024]{1,0:T(8,128)(2,1)S(1)}, bf16[96,1024]{1,0:T(8,128)(2,1)S(1)}, u32[]{:S(2)}, u32[]{:S(2)}) collective-permute-start(bf16[96,1024]{1,0:T(8,128)(2,1)S(1)} %get-tuple-element.58), channel_id=1, source_target_pairs={{0,192},{64,0},{128,64},{192,128},{1,193},{65,1},{129,65},{193,129... | collective-permute-start | bytes 589832 | tf_op jit(solution)/shard_map/ppermute | solution.py:347
  14.1 8.1 %collective-permute-start.8 = (bf16[96,1024]{1,0:T(8,128)(2,1)S(1)}, bf16[96,1024]{1,0:T(8,128)(2,1)S(1)}, u32[]{:S(2)}, u32[]{:S(2)}) collective-permute-start(bf16[96,1024]{1,0:T(8,128)(2,1)S(1)} %get-tuple-element.58), channel_id=1, source_target_pairs={{0,64},{64,128},{128,192},{192,0},{1,65},{65,129},{129,193},{193,1... | collective-permute-start | bytes 589832 | tf_op jit(solution)/shard_map/ppermute | solution.py:346
  18.0 6.8 %collective-permute-start.1 = (bf16[48,1024]{1,0:T(8,128)(2,1)S(1)}, bf16[48,1024]{1,0:T(8,128)(2,1)S(1)}, u32[]{:S(2)}, u32[]{:S(2)}) collective-permute-start(bf16[48,1024]{1,0:T(8,128)(2,1)S(1)} %slice.193), channel_id=1, source_target_pairs={{0,16},{16,32},{32,48},{48,0},{1,17},{17,33},{33,49},{49,1},{2,18}... | collective-permute-start | bytes 294920 | tf_op jit(solution)/shard_map/ppermute | solution.py:348
  18.4 6.5 %collective-permute-start.3 = (bf16[48,1024]{1,0:T(8,128)(2,1)S(1)}, bf16[48,1024]{1,0:T(8,128)(2,1)S(1)}, u32[]{:S(2)}, u32[]{:S(2)}) collective-permute-start(bf16[48,1024]{1,0:T(8,128)(2,1)S(1)} %slice.194), channel_id=1, source_target_pairs={{0,48},{16,0},{32,16},{48,32},{1,49},{17,1},{33,17},{49,33},{2,50}... | collective-permute-start | bytes 294920 | tf_op jit(solution)/shard_map/ppermute | solution.py:349
  21.4 6.5 %collective-permute-start.11 = (bf16[48,1024]{1,0:T(8,128)(2,1)S(1)}, bf16[48,1024]{1,0:T(8,128)(2,1)S(1)}, u32[]{:S(2)}, u32[]{:S(2)}) collective-permute-start(bf16[48,1024]{1,0:T(8,128)(2,1)S(1)} %slice.199), channel_id=1, source_target_pairs={{0,192},{64,0},{128,64},{192,128},{1,193},{65,1},{129,65},{193,129... | collective-permute-start | bytes 294920 | tf_op jit(solution)/shard_map/ppermute | solution.py:349
  22.3 5.8 %collective-permute-start.9 = (bf16[48,1024]{1,0:T(8,128)(2,1)S(1)}, bf16[48,1024]{1,0:T(8,128)(2,1)S(1)}, u32[]{:S(2)}, u32[]{:S(2)}) collective-permute-start(bf16[48,1024]{1,0:T(8,128)(2,1)S(1)} %slice.198), channel_id=1, source_target_pairs={{0,64},{64,128},{128,192},{192,0},{1,65},{65,129},{129,193},{193,1... | collective-permute-start | bytes 294920 | tf_op jit(solution)/shard_map/ppermute | solution.py:348
  25.0 23.0 %copy-start.3 = (bf16[4,96,1024]{2,1,0:T(8,128)(2,1)}, bf16[4,96,1024]{2,1,0:T(8,128)(2,1)S(1)}, u32[]{:S(2)}) copy-start(bf16[4,96,1024]{2,1,0:T(8,128)(2,1)S(1)} %pad_maximum_fusion.own_ref) | copy-start | bytes 2359300
  25.0 18.5 %collective-permute-start.4 = (bf16[4,96,1024]{2,1,0:T(8,128)(2,1)S(1)}, bf16[4,96,1024]{2,1,0:T(8,128)(2,1)}, u32[]{:S(2)}, u32[]{:S(2)}) collective-permute-start(bf16[4,96,1024]{2,1,0:T(8,128)(2,1)S(1)} %pad_maximum_fusion.own_ref), channel_id=1, source_target_pairs={{0,64},{64,128},{128,192},{192,0},{1,65},{65,129},{129,193},{193,1... | collective-permute-start | bytes 2359304 | tf_op jit(solution)/shard_map/ppermute | solution.py:346
  25.1 21.8 %collective-permute-start.5 = (bf16[4,96,1024]{2,1,0:T(8,128)(2,1)S(1)}, bf16[4,96,1024]{2,1,0:T(8,128)(2,1)}, u32[]{:S(2)}, u32[]{:S(2)}) collective-permute-start(bf16[4,96,1024]{2,1,0:T(8,128)(2,1)S(1)} %pad_maximum_fusion.own_ref), channel_id=1, source_target_pairs={{0,192},{64,0},{128,64},{192,128},{1,193},{65,1},{129,65},{193,129... | collective-permute-start | bytes 2359304 | tf_op jit(solution)/shard_map/ppermute | solution.py:347
  28.2 21.2 %copy-start.2 = (bf16[4,96,1024]{2,1,0:T(8,128)(2,1)}, bf16[4,96,1024]{2,1,0:T(8,128)(2,1)S(1)}, u32[]{:S(2)}) copy-start(bf16[4,96,1024]{2,1,0:T(8,128)(2,1)S(1)} %pad_maximum_fusion.1.own_ref) | copy-start | bytes 2359300
  28.2 19.8 %collective-permute-start.12 = (bf16[4,96,1024]{2,1,0:T(8,128)(2,1)S(1)}, bf16[4,96,1024]{2,1,0:T(8,128)(2,1)S(1)}, u32[]{:S(2)}, u32[]{:S(2)}) collective-permute-start(bf16[4,96,1024]{2,1,0:T(8,128)(2,1)S(1)} %pad_maximum_fusion.1.own_ref), channel_id=1, source_target_pairs={{0,16},{16,32},{32,48},{48,0},{1,17},{17,33},{33,49},{49,1},{2,18}... | collective-permute-start | bytes 2359304 | tf_op jit(solution)/shard_map/ppermute | solution.py:346
  28.3 20.1 %collective-permute-start.13 = (bf16[4,96,1024]{2,1,0:T(8,128)(2,1)S(1)}, bf16[4,96,1024]{2,1,0:T(8,128)(2,1)}, u32[]{:S(2)}, u32[]{:S(2)}) collective-permute-start(bf16[4,96,1024]{2,1,0:T(8,128)(2,1)S(1)} %pad_maximum_fusion.1.own_ref), channel_id=1, source_target_pairs={{0,48},{16,0},{32,16},{48,32},{1,49},{17,1},{33,17},{49,33},{2,50}... | collective-permute-start | bytes 2359304 | tf_op jit(solution)/shard_map/ppermute | solution.py:347
  44.5 35.4 %collective-permute-start.6 = (bf16[2,96,1024]{2,1,0:T(8,128)(2,1)S(1)}, bf16[2,96,1024]{2,1,0:T(8,128)(2,1)}, u32[]{:S(2)}, u32[]{:S(2)}) collective-permute-start(bf16[2,96,1024]{2,1,0:T(8,128)(2,1)S(1)} %slice.195), channel_id=1, source_target_pairs={{0,64},{64,128},{128,192},{192,0},{1,65},{65,129},{129,193},{193,1... | collective-permute-start | bytes 1179656 | tf_op jit(solution)/shard_map/ppermute | solution.py:348
  48.0 31.9 %collective-permute-start.7 = (bf16[2,96,1024]{2,1,0:T(8,128)(2,1)S(1)}, bf16[2,96,1024]{2,1,0:T(8,128)(2,1)}, u32[]{:S(2)}, u32[]{:S(2)}) collective-permute-start(bf16[2,96,1024]{2,1,0:T(8,128)(2,1)S(1)} %slice.196), channel_id=1, source_target_pairs={{0,192},{64,0},{128,64},{192,128},{1,193},{65,1},{129,65},{193,129... | collective-permute-start | bytes 1179656 | tf_op jit(solution)/shard_map/ppermute | solution.py:349
  48.1 31.8 %copy-start.10 = (bf16[4,96,1024]{2,1,0:T(8,128)(2,1)}, bf16[4,96,1024]{2,1,0:T(8,128)(2,1)S(1)}, u32[]{:S(2)}) copy-start(bf16[4,96,1024]{2,1,0:T(8,128)(2,1)S(1)} %collective-permute-done.12.from_down_ref) | copy-start | bytes 2359300
  48.1 48.6 %collective-permute-start.14 = (bf16[2,96,1024]{2,1,0:T(8,128)(2,1)S(1)}, bf16[2,96,1024]{2,1,0:T(8,128)(2,1)}, u32[]{:S(2)}, u32[]{:S(2)}) collective-permute-start(bf16[2,96,1024]{2,1,0:T(8,128)(2,1)S(1)} %slice.200), channel_id=1, source_target_pairs={{0,16},{16,32},{32,48},{48,0},{1,17},{17,33},{33,49},{49,1},{2,18}... | collective-permute-start | bytes 1179656 | tf_op jit(solution)/shard_map/ppermute | solution.py:348
  49.4 47.3 %collective-permute-start.15 = (bf16[2,96,1024]{2,1,0:T(8,128)(2,1)S(1)}, bf16[2,96,1024]{2,1,0:T(8,128)(2,1)}, u32[]{:S(2)}, u32[]{:S(2)}) collective-permute-start(bf16[2,96,1024]{2,1,0:T(8,128)(2,1)S(1)} %slice.201), channel_id=1, source_target_pairs={{0,48},{16,0},{32,16},{48,32},{1,49},{17,1},{33,17},{49,33},{2,50}... | collective-permute-start | bytes 1179656 | tf_op jit(solution)/shard_map/ppermute | solution.py:349
  94.6 40.4 %collective-permute-start.16 = (bf16[2,96,1024]{2,1,0:T(8,128)(2,1)}, bf16[2,96,1024]{2,1,0:T(8,128)(2,1)}, u32[]{:S(2)}, u32[]{:S(2)}) collective-permute-start(bf16[2,96,1024]{2,1,0:T(8,128)(2,1)} %get-tuple-element.32), channel_id=1, source_target_pairs={{0,64},{64,128},{128,192},{192,0},{1,65},{65,129},{129,193},{193,1... | collective-permute-start | bytes 1179656 | tf_op jit(solution)/shard_map/ppermute | solution.py:366
  95.2 43.2 %collective-permute-start.18 = (bf16[2,96,1024]{2,1,0:T(8,128)(2,1)}, bf16[2,96,1024]{2,1,0:T(8,128)(2,1)S(1)}, u32[]{:S(2)}, u32[]{:S(2)}) collective-permute-start(bf16[2,96,1024]{2,1,0:T(8,128)(2,1)} %get-tuple-element.34), channel_id=1, source_target_pairs={{0,192},{64,0},{128,64},{192,128},{1,193},{65,1},{129,65},{193,129... | collective-permute-start | bytes 1179656 | tf_op jit(solution)/shard_map/ppermute | solution.py:367
  111.4 27.6 %collective-permute-start.24 = (bf16[2,96,1024]{2,1,0:T(8,128)(2,1)}, bf16[2,96,1024]{2,1,0:T(8,128)(2,1)}, u32[]{:S(2)}, u32[]{:S(2)}) collective-permute-start(bf16[2,96,1024]{2,1,0:T(8,128)(2,1)} %get-tuple-element.37), channel_id=1, source_target_pairs={{0,16},{16,32},{32,48},{48,0},{1,17},{17,33},{33,49},{49,1},{2,18}... | collective-permute-start | bytes 1179656 | tf_op jit(solution)/shard_map/ppermute | solution.py:366
  112.9 27.6 %collective-permute-start.26 = (bf16[2,96,1024]{2,1,0:T(8,128)(2,1)}, bf16[2,96,1024]{2,1,0:T(8,128)(2,1)}, u32[]{:S(2)}, u32[]{:S(2)}) collective-permute-start(bf16[2,96,1024]{2,1,0:T(8,128)(2,1)} %get-tuple-element.39), channel_id=1, source_target_pairs={{0,48},{16,0},{32,16},{48,32},{1,49},{17,1},{33,17},{49,33},{2,50}... | collective-permute-start | bytes 1179656 | tf_op jit(solution)/shard_map/ppermute | solution.py:367
  131.1 2.4 %copy-start.6 = (bf16[4,96,1024]{2,1,0:T(8,128)(2,1)S(1)}, bf16[4,96,1024]{2,1,0:T(8,128)(2,1)}, u32[]{:S(2)}) copy-start(bf16[4,96,1024]{2,1,0:T(8,128)(2,1)} %get-tuple-element.31) | copy-start | bytes 2359300
  131.1 2.5 %copy-start.4 = (bf16[4,96,1024]{2,1,0:T(8,128)(2,1)S(1)}, bf16[4,96,1024]{2,1,0:T(8,128)(2,1)}, u32[]{:S(2)}) copy-start(bf16[4,96,1024]{2,1,0:T(8,128)(2,1)} %get-tuple-element.33) | copy-start | bytes 2359300
  133.6 1.1 copy-start.7
  133.6 1.4 copy-start.5
  136.3 2.6 %copy-start.8 = (bf16[4,96,1024]{2,1,0:T(8,128)(2,1)S(1)}, bf16[4,96,1024]{2,1,0:T(8,128)(2,1)}, u32[]{:S(2)}) copy-start(bf16[4,96,1024]{2,1,0:T(8,128)(2,1)} %get-tuple-element.36) | copy-start | bytes 2359300
  136.4 19.9 %collective-permute-start.17 = (bf16[4,96,1024]{2,1,0:T(8,128)(2,1)S(1)}, bf16[4,96,1024]{2,1,0:T(8,128)(2,1)S(1)}, u32[]{:S(2)}, u32[]{:S(2)}) collective-permute-start(bf16[4,96,1024]{2,1,0:T(8,128)(2,1)S(1)} %pad_maximum_fusion.2), channel_id=1, source_target_pairs={{0,64},{64,128},{128,192},{192,0},{1,65},{65,129},{129,193},{193,1... | collective-permute-start | bytes 2359304 | tf_op jit(solution)/shard_map/ppermute | solution.py:370
  138.6 20.6 %collective-permute-start.19 = (bf16[4,96,1024]{2,1,0:T(8,128)(2,1)S(1)}, bf16[4,96,1024]{2,1,0:T(8,128)(2,1)S(1)}, u32[]{:S(2)}, u32[]{:S(2)}) collective-permute-start(bf16[4,96,1024]{2,1,0:T(8,128)(2,1)S(1)} %pad_maximum_fusion.3), channel_id=1, source_target_pairs={{0,192},{64,0},{128,64},{192,128},{1,193},{65,1},{129,65},{193,129... | collective-permute-start | bytes 2359304 | tf_op jit(solution)/shard_map/ppermute | solution.py:371
  140.2 19.0 %copy-start = (bf16[4,96,1024]{2,1,0:T(8,128)(2,1)S(1)}, bf16[4,96,1024]{2,1,0:T(8,128)(2,1)}, u32[]{:S(2)}) copy-start(bf16[4,96,1024]{2,1,0:T(8,128)(2,1)} %get-tuple-element.30) | copy-start | bytes 2359300
  140.2 22.8 %collective-permute-start.25 = (bf16[4,96,1024]{2,1,0:T(8,128)(2,1)S(1)}, bf16[4,96,1024]{2,1,0:T(8,128)(2,1)S(1)}, u32[]{:S(2)}, u32[]{:S(2)}) collective-permute-start(bf16[4,96,1024]{2,1,0:T(8,128)(2,1)S(1)} %pad_maximum_fusion.4), channel_id=1, source_target_pairs={{0,16},{16,32},{32,48},{48,0},{1,17},{17,33},{33,49},{49,1},{2,18}... | collective-permute-start | bytes 2359304 | tf_op jit(solution)/shard_map/ppermute | solution.py:370
  141.8 21.2 %collective-permute-start.27 = (bf16[4,96,1024]{2,1,0:T(8,128)(2,1)S(1)}, bf16[4,96,1024]{2,1,0:T(8,128)(2,1)S(1)}, u32[]{:S(2)}, u32[]{:S(2)}) collective-permute-start(bf16[4,96,1024]{2,1,0:T(8,128)(2,1)S(1)} %pad_maximum_fusion.5), channel_id=1, source_target_pairs={{0,48},{16,0},{32,16},{48,32},{1,49},{17,1},{33,17},{49,33},{2,50}... | collective-permute-start | bytes 2359304 | tf_op jit(solution)/shard_map/ppermute | solution.py:371
  159.2 3.8 %copy-start.1 = (bf16[4,96,1024]{2,1,0:T(8,128)(2,1)S(1)}, bf16[4,96,1024]{2,1,0:T(8,128)(2,1)}, u32[]{:S(2)}) copy-start(bf16[4,96,1024]{2,1,0:T(8,128)(2,1)} %get-tuple-element.35) | copy-start | bytes 2359300
  159.7 6.0 %collective-permute-start.20 = (bf16[48,1024]{1,0:T(8,128)(2,1)S(1)}, bf16[48,1024]{1,0:T(8,128)(2,1)S(1)}, u32[]{:S(2)}, u32[]{:S(2)}) collective-permute-start(bf16[48,1024]{1,0:T(8,128)(2,1)S(1)} %get-tuple-element.46), channel_id=1, source_target_pairs={{0,16},{16,32},{32,48},{48,0},{1,17},{17,33},{33,49},{49,1},{2,18}... | collective-permute-start | bytes 294920 | tf_op jit(solution)/shard_map/ppermute | solution.py:366
  160.0 5.6 %collective-permute-start.22 = (bf16[48,1024]{1,0:T(8,128)(2,1)S(1)}, bf16[48,1024]{1,0:T(8,128)(2,1)S(1)}, u32[]{:S(2)}, u32[]{:S(2)}) collective-permute-start(bf16[48,1024]{1,0:T(8,128)(2,1)S(1)} %get-tuple-element.47), channel_id=1, source_target_pairs={{0,48},{16,0},{32,16},{48,32},{1,49},{17,1},{33,17},{49,33},{2,50}... | collective-permute-start | bytes 294920 | tf_op jit(solution)/shard_map/ppermute | solution.py:367
  163.5 6.1 %collective-permute-start.28 = (bf16[48,1024]{1,0:T(8,128)(2,1)S(1)}, bf16[48,1024]{1,0:T(8,128)(2,1)S(1)}, u32[]{:S(2)}, u32[]{:S(2)}) collective-permute-start(bf16[48,1024]{1,0:T(8,128)(2,1)S(1)} %get-tuple-element.52), channel_id=1, source_target_pairs={{0,64},{64,128},{128,192},{192,0},{1,65},{65,129},{129,193},{193,1... | collective-permute-start | bytes 294920 | tf_op jit(solution)/shard_map/ppermute | solution.py:366
  165.6 5.8 %collective-permute-start.30 = (bf16[48,1024]{1,0:T(8,128)(2,1)S(1)}, bf16[48,1024]{1,0:T(8,128)(2,1)S(1)}, u32[]{:S(2)}, u32[]{:S(2)}) collective-permute-start(bf16[48,1024]{1,0:T(8,128)(2,1)S(1)} %get-tuple-element.53), channel_id=1, source_target_pairs={{0,192},{64,0},{128,64},{192,128},{1,193},{65,1},{129,65},{193,129... | collective-permute-start | bytes 294920 | tf_op jit(solution)/shard_map/ppermute | solution.py:367
  165.7 8.0 %collective-permute-start.21 = (bf16[96,1024]{1,0:T(8,128)(2,1)S(1)}, bf16[96,1024]{1,0:T(8,128)(2,1)S(1)}, u32[]{:S(2)}, u32[]{:S(2)}) collective-permute-start(bf16[96,1024]{1,0:T(8,128)(2,1)S(1)} %pad_maximum_fusion.8), channel_id=1, source_target_pairs={{0,16},{16,32},{32,48},{48,0},{1,17},{17,33},{33,49},{49,1},{2,18}... | collective-permute-start | bytes 589832 | tf_op jit(solution)/shard_map/ppermute | solution.py:370
  166.8 7.0 %collective-permute-start.23 = (bf16[96,1024]{1,0:T(8,128)(2,1)S(1)}, bf16[96,1024]{1,0:T(8,128)(2,1)S(1)}, u32[]{:S(2)}, u32[]{:S(2)}) collective-permute-start(bf16[96,1024]{1,0:T(8,128)(2,1)S(1)} %pad_maximum_fusion.9), channel_id=1, source_target_pairs={{0,48},{16,0},{32,16},{48,32},{1,49},{17,1},{33,17},{49,33},{2,50}... | collective-permute-start | bytes 589832 | tf_op jit(solution)/shard_map/ppermute | solution.py:371
  171.5 5.7 %collective-permute-start.29 = (bf16[96,1024]{1,0:T(8,128)(2,1)S(1)}, bf16[96,1024]{1,0:T(8,128)(2,1)S(1)}, u32[]{:S(2)}, u32[]{:S(2)}) collective-permute-start(bf16[96,1024]{1,0:T(8,128)(2,1)S(1)} %pad_maximum_fusion.10), channel_id=1, source_target_pairs={{0,64},{64,128},{128,192},{192,0},{1,65},{65,129},{129,193},{193,1... | collective-permute-start | bytes 589832 | tf_op jit(solution)/shard_map/ppermute | solution.py:370
  173.0 7.0 %collective-permute-start.31 = (bf16[96,1024]{1,0:T(8,128)(2,1)S(1)}, bf16[96,1024]{1,0:T(8,128)(2,1)S(1)}, u32[]{:S(2)}, u32[]{:S(2)}) collective-permute-start(bf16[96,1024]{1,0:T(8,128)(2,1)S(1)} %pad_maximum_fusion.11), channel_id=1, source_target_pairs={{0,192},{64,0},{128,64},{192,128},{1,193},{65,1},{129,65},{193,129... | collective-permute-start | bytes 589832 | tf_op jit(solution)/shard_map/ppermute | solution.py:371
Sparse Core Ops, SparseCore 0:
  10.0 59.8 all-gather.2
  135.1 39.9 reduce-scatter.1
